TPU v7x, 512 devices: a whole 4x4x16 slice. The times are simulated.
512 devices in a mesh: lat: 16 (over x_lo, y, core), lon: 32 (over x_hi, z).
Axes of the slice: x: 4 (x_hi: 2, x_lo: 2; x = x_hi * 2 + x_lo), y: 4, z: 16, core: 2. Of those that a mesh axis runs over, the one named last changes fastest.
Arguments:
- field: float32 [256, 16, 4096], P(None, 'lat', 'lon'), may hold values from -6 to 6
- cotangent: float32 [256, 16, 4096], P(None, 'lat', 'lon'), may hold values from -6 to 6
- conv_weight: float32 [3, 3, 256, 256], replicated, may hold values from -0.125 to 0.125
- spectral_filter: float32 [2, 256, 4096], P(None, None, 'lon'), may hold values from -6 to 6
Outputs:
- output: float32 [256, 16, 4096], P(None, 'lat', 'lon')
- input_grad: float32 [256, 16, 4096], P(None, 'lat', 'lon')
- filter_grad: float32 [2, 256, 4096], P(None, None, 'lon')
All inputs are finite; a program needn't handle non-finite values.
Results may differ from a plain program's by a relative error of at most 0.00014.
Values sent between devices are 32-bit elements; how exact they have to be, the bound alone decides.
A program may use at most 64 MiB of HBM per device.

v0:
```python
import jax
import jax.numpy as jnp
from jax import lax
from jax.sharding import PartitionSpec as P

precise = lax.Precision.HIGHEST


def padded_2(array, sides, width, wrap):
    for axis, dim in sides:
        peers, length = (lax.axis_size(axis), array.shape[dim])
        up = [(i, (i + 1) % peers) for i in range(peers if wrap else peers - 1)]
        down = [(j, i) for i, j in up]
        last = lax.slice_in_dim(array, length - width, length, axis=dim)
        leading = lax.slice_in_dim(array, 0, width, axis=dim)
        before = lax.ppermute(last, axis, up)
        after = lax.ppermute(leading, axis, down)
        array = jnp.concatenate([before, array, after], axis=dim)
    return array


def partner(array, axis, stride):
    return lax.ppermute(array, axis, [(i, i ^ 1 << stride) for i in range(lax.axis_size(axis))])


def angle_table(first, second, modulus):
    product = first[:, None] * second[None, :] % modulus
    return 2.0 * jnp.pi / modulus * product.astype(jnp.float32)


def apply_taps(padded, taps, lat_rows, columns):
    total = jnp.zeros((taps.shape[2], lat_rows, columns), jnp.float32)
    for tap_row in range(3):
        for tap_col in range(3):
            window = padded[:, tap_row : tap_row + lat_rows, tap_col : tap_col + columns]
            total = total + jnp.einsum(
                "oi,iab->oab", taps[tap_row, tap_col], window, precision=precise
            )
    return total


def with_rims(field):
    wider = padded_2(field, (("lon", 2),), 1, True)
    return padded_2(wider, (("lat", 1),), 1, False)


def local_forward(real_part, imag_part):
    columns = real_part.shape[-1]
    places = lax.iota(jnp.int32, columns)
    angles = angle_table(places, places, columns)
    cosine = jnp.cos(angles)
    sine = jnp.sin(angles)
    out_real = jnp.dot(real_part, cosine, precision=precise) + jnp.dot(
        imag_part, sine, precision=precise
    )
    out_imag = jnp.dot(imag_part, cosine, precision=precise) - jnp.dot(
        real_part, sine, precision=precise
    )
    return (out_real, out_imag)


def local_inverse(real_part, imag_part):
    columns = real_part.shape[-1]
    places = lax.iota(jnp.int32, columns)
    angles = angle_table(places, places, columns)
    cosine = jnp.cos(angles)
    sine = jnp.sin(angles)
    out_real = jnp.dot(real_part, cosine, precision=precise) - jnp.dot(
        imag_part, sine, precision=precise
    )
    out_imag = jnp.dot(imag_part, cosine, precision=precise) + jnp.dot(
        real_part, sine, precision=precise
    )
    return (out_real / columns, out_imag / columns)


def section_angles(place, bit_pos, columns):
    offsets = lax.iota(jnp.int32, columns)
    start = place % 2**bit_pos * columns
    span = 2 * columns * 2**bit_pos
    angles = 2.0 * jnp.pi / span * (start + offsets).astype(jnp.float32)
    upper = place // 2**bit_pos % 2 == 1
    return (jnp.cos(angles), jnp.sin(angles), upper)


def forward_pairs(field):
    extent = lax.axis_size("lon")
    width_bits = extent.bit_length() - 1
    place = lax.axis_index("lon")
    columns = field.shape[-1]
    data = jnp.stack([field, jnp.zeros_like(field)])
    for bit_pos in reversed(range(width_bits)):
        other = partner(data, "lon", bit_pos)
        cosine, sine, upper = section_angles(place, bit_pos, columns)
        differ = other - data
        turned = jnp.stack(
            [differ[0] * cosine + differ[1] * sine, differ[1] * cosine - differ[0] * sine]
        )
        data = jnp.where(upper, turned, data + other)
    out_real, out_imag = local_forward(data[0], data[1])
    return jnp.stack([out_real, out_imag])


def inverse_pairs(spectrum):
    extent = lax.axis_size("lon")
    width_bits = extent.bit_length() - 1
    place = lax.axis_index("lon")
    columns = spectrum.shape[-1]
    back_real, back_imag = local_inverse(spectrum[0], spectrum[1])
    data = jnp.stack([back_real, back_imag])
    for bit_pos in range(width_bits):
        cosine, sine, upper = section_angles(place, bit_pos, columns)
        turned = jnp.stack([data[0] * cosine - data[1] * sine, data[1] * cosine + data[0] * sine])
        outgoing = jnp.where(upper, turned, data)
        other = partner(outgoing, "lon", bit_pos)
        data = jnp.where(upper, other - outgoing, outgoing + other) * 0.5
    return data[0]


def on_device(field, cotangent, conv_weight, spectral_filter):
    lat_rows = field.shape[1]
    columns = field.shape[2]
    total_len = columns * lax.axis_size("lon")
    mixed = apply_taps(with_rims(field), conv_weight, lat_rows, columns)
    hidden_spec = forward_pairs(mixed)
    cot_spec = forward_pairs(cotangent)
    gain_real = spectral_filter[0][:, None, :]
    gain_imag = spectral_filter[1][:, None, :]
    filtered = jnp.stack(
        [
            gain_real * hidden_spec[0] - gain_imag * hidden_spec[1],
            gain_real * hidden_spec[1] + gain_imag * hidden_spec[0],
        ]
    )
    adjoint = jnp.stack(
        [
            gain_real * cot_spec[0] + gain_imag * cot_spec[1],
            gain_real * cot_spec[1] - gain_imag * cot_spec[0],
        ]
    )
    shaped = inverse_pairs(filtered)
    back_field = inverse_pairs(adjoint)
    output = field + shaped
    local_grad = (
        jnp.stack(
            [
                jnp.sum(hidden_spec[0] * cot_spec[0] + hidden_spec[1] * cot_spec[1], axis=1),
                jnp.sum(hidden_spec[0] * cot_spec[1] - hidden_spec[1] * cot_spec[0], axis=1),
            ]
        )
        / total_len
    )
    filter_grad = lax.psum(local_grad, "lat")
    flipped_taps = jnp.transpose(conv_weight[::-1, ::-1], (0, 1, 3, 2))
    input_grad = cotangent + apply_taps(with_rims(back_field), flipped_taps, lat_rows, columns)
    return (output, input_grad, filter_grad)


def solution(mesh):
    placed = (P(None, "lat", "lon"), P(None, "lat", "lon"), P(), P(None, None, "lon"))
    return jax.shard_map(
        on_device,
        mesh=mesh,
        in_specs=placed,
        out_specs=(P(None, "lat", "lon"), P(None, "lat", "lon"), P(None, None, "lon")),
        check_vma=False,
    )
```

profile of v0, /device:TPU:1, one launch (start us, length us, event | category | flops | bytes accessed | tf_op | source)
XLA Modules:
  0.0 503.1 jit_solution(4956193246249797645)
XLA Ops:
  13.1 12.0 %collective-permute-start.1 = (f32[256,1,1]{2,1,0:T(1,128)S(1)}, f32[256,1,1]{2,1,0:T(1,128)S(1)}, u32[]{:S(2)}, u32[]{:S(2)}) collective-permute-start(f32[256,1,1]{2,1,0:T(1,128)S(1)} %get-tuple-element.71), channel_id=1, source_target_pairs={{1,0},{2,1},{3,2},{4,3},{5,4},{6,5},{7,6},{8,7},{9,8},{10,9},{11,1... | collective-permute-start | bytes 3080 | tf_op jit(solution)/shard_map/ppermute | solution.py:17
  43.8 4.6 collective-permute-start.4
  48.6 6.7 %collective-permute-done.4 = f32[2,256,1,128]{1,3,2,0:T(8,128)S(1)} collective-permute-done((f32[2,256,1,128]{1,3,2,0:T(8,128)}, f32[2,256,1,128]{1,3,2,0:T(8,128)S(1)}, u32[]{:S(2)}, u32[]{:S(2)}) %collective-permute-start.4) | collective-permute-done | bytes 262176 | tf_op jit(solution)/shard_map/ppermute | solution.py:23
  56.4 9.2 %collective-permute-start.5 = (f32[2,256,1,128]{1,3,2,0:T(8,128)}, f32[2,256,1,128]{1,3,2,0:T(8,128)}, u32[]{:S(2)}, u32[]{:S(2)}) collective-permute-start(f32[2,256,1,128]{1,3,2,0:T(8,128)} %maximum_select_fusion), channel_id=1, source_target_pairs={{0,8},{1,9},{2,10},{3,11},{4,12},{5,13},{6,14},{7,15},{8,0},{9,1},... | collective-permute-start | bytes 786440 | tf_op jit(solution)/shard_map/ppermute | solution.py:23
  66.4 4.8 collective-permute-start.15
  71.2 20.3 %collective-permute-done.5 = f32[2,256,1,128]{1,3,2,0:T(8,128)} collective-permute-done((f32[2,256,1,128]{1,3,2,0:T(8,128)}, f32[2,256,1,128]{1,3,2,0:T(8,128)}, u32[]{:S(2)}, u32[]{:S(2)}) %collective-permute-start.5) | collective-permute-done | bytes 262176 | tf_op jit(solution)/shard_map/ppermute | solution.py:23
  92.5 20.8 %collective-permute-done.15 = f32[2,256,1,128]{1,3,2,0:T(8,128)} collective-permute-done((f32[2,256,1,128]{1,3,2,0:T(8,128)}, f32[2,256,1,128]{1,3,2,0:T(8,128)}, u32[]{:S(2)}, u32[]{:S(2)}) %collective-permute-start.15) | collective-permute-done | bytes 262176 | tf_op jit(solution)/shard_map/ppermute | solution.py:23
  118.7 7.3 %collective-permute-start.6 = (f32[2,256,1,128]{1,3,2,0:T(8,128)S(1)}, f32[2,256,1,128]{1,3,2,0:T(8,128)}, u32[]{:S(2)}, u32[]{:S(2)}) collective-permute-start(f32[2,256,1,128]{1,3,2,0:T(8,128)S(1)} %maximum_select_fusion.1), channel_id=1, source_target_pairs={{0,4},{1,5},{2,6},{3,7},{4,0},{5,1},{6,2},{7,3},{8,12},{9,13},{10,... | collective-permute-start | bytes 786440 | tf_op jit(solution)/shard_map/ppermute | solution.py:23
  126.1 30.2 %collective-permute-done.16 = f32[2,256,1,128]{1,3,2,0:T(8,128)} collective-permute-done((f32[2,256,1,128]{1,3,2,0:T(8,128)S(1)}, f32[2,256,1,128]{1,3,2,0:T(8,128)}, u32[]{:S(2)}, u32[]{:S(2)}) %collective-permute-start.16) | collective-permute-done | bytes 262176 | tf_op jit(solution)/shard_map/ppermute | solution.py:23
  157.3 4.6 collective-permute-done.6
  171.3 10.2 %collective-permute-done.17 = f32[2,256,1,128]{1,3,2,0:T(8,128)} collective-permute-done((f32[2,256,1,128]{1,3,2,0:T(8,128)S(1)}, f32[2,256,1,128]{1,3,2,0:T(8,128)}, u32[]{:S(2)}, u32[]{:S(2)}) %collective-permute-start.17) | collective-permute-done | bytes 262176 | tf_op jit(solution)/shard_map/ppermute | solution.py:23
  223.6 5.6 %collective-permute-done.9 = f32[2,256,1,128]{1,3,2,0:T(8,128)S(1)} collective-permute-done((f32[2,256,1,128]{1,3,2,0:T(8,128)S(1)}, f32[2,256,1,128]{1,3,2,0:T(8,128)S(1)}, u32[]{:S(2)}, u32[]{:S(2)}) %collective-permute-start.9) | collective-permute-done | bytes 262176 | tf_op jit(solution)/shard_map/ppermute | solution.py:23
  235.7 15.6 %collective-permute-done.10 = f32[2,256,1,128]{1,3,2,0:T(8,128)S(1)} collective-permute-done((f32[2,256,1,128]{1,3,2,0:T(8,128)S(1)}, f32[2,256,1,128]{1,3,2,0:T(8,128)S(1)}, u32[]{:S(2)}, u32[]{:S(2)}) %collective-permute-start.10) | collective-permute-done | bytes 262176 | tf_op jit(solution)/shard_map/ppermute | solution.py:23
  251.4 5.6 %collective-permute-done.20 = f32[2,256,1,128]{1,3,2,0:T(8,128)S(1)} collective-permute-done((f32[2,256,1,128]{1,3,2,0:T(8,128)S(1)}, f32[2,256,1,128]{1,3,2,0:T(8,128)S(1)}, u32[]{:S(2)}, u32[]{:S(2)}) %collective-permute-start.20) | collective-permute-done | bytes 262176 | tf_op jit(solution)/shard_map/ppermute | solution.py:23
  261.1 5.4 %collective-permute-start.21 = (f32[2,256,1,128]{1,3,2,0:T(8,128)S(1)}, f32[2,256,1,128]{1,3,2,0:T(8,128)S(1)}, u32[]{:S(2)}, u32[]{:S(2)}) collective-permute-start(f32[2,256,1,128]{1,3,2,0:T(8,128)S(1)} %maximum_select_fusion.17), channel_id=1, source_target_pairs={{0,4},{1,5},{2,6},{3,7},{4,0},{5,1},{6,2},{7,3},{8,12},{9,13},{10,... | collective-permute-start | bytes 786440 | tf_op jit(solution)/shard_map/ppermute | solution.py:23
  266.4 35.6 %collective-permute-done.11 = f32[2,256,1,128]{1,3,2,0:T(8,128)S(1)} collective-permute-done((f32[2,256,1,128]{1,3,2,0:T(8,128)S(1)}, f32[2,256,1,128]{1,3,2,0:T(8,128)S(1)}, u32[]{:S(2)}, u32[]{:S(2)}) %collective-permute-start.11) | collective-permute-done | bytes 262176 | tf_op jit(solution)/shard_map/ppermute | solution.py:23
  302.1 16.9 %collective-permute-done.21 = f32[2,256,1,128]{1,3,2,0:T(8,128)S(1)} collective-permute-done((f32[2,256,1,128]{1,3,2,0:T(8,128)S(1)}, f32[2,256,1,128]{1,3,2,0:T(8,128)S(1)}, u32[]{:S(2)}, u32[]{:S(2)}) %collective-permute-start.21) | collective-permute-done | bytes 262176 | tf_op jit(solution)/shard_map/ppermute | solution.py:23
  320.6 10.3 %collective-permute-start.12 = (f32[2,256,1,128]{1,3,2,0:T(8,128)}, f32[2,256,1,128]{1,3,2,0:T(8,128)}, u32[]{:S(2)}, u32[]{:S(2)}) collective-permute-start(f32[2,256,1,128]{1,3,2,0:T(8,128)} %maximum_select_fusion.8), channel_id=1, source_target_pairs={{0,8},{1,9},{2,10},{3,11},{4,12},{5,13},{6,14},{7,15},{8,0},{9,1},... | collective-permute-start | bytes 786440 | tf_op jit(solution)/shard_map/ppermute | solution.py:23
  337.7 4.7 collective-permute-done.12
  343.6 6.0 %collective-permute-done.22 = f32[2,256,1,128]{1,3,2,0:T(8,128)} collective-permute-done((f32[2,256,1,128]{1,3,2,0:T(8,128)}, f32[2,256,1,128]{1,3,2,0:T(8,128)}, u32[]{:S(2)}, u32[]{:S(2)}) %collective-permute-start.22) | collective-permute-done | bytes 262176 | tf_op jit(solution)/shard_map/ppermute | solution.py:23
  353.5 4.9 collective-permute-start.13
  363.1 8.9 %collective-permute-start.25 = (f32[256,1,1]{0,2,1:T(1,128)S(1)}, f32[256,1,1]{0,2,1:T(1,128)S(1)}, u32[]{:S(2)}, u32[]{:S(2)}) collective-permute-start(f32[256,1,1]{0,2,1:T(1,128)S(1)} %get-tuple-element.63), channel_id=1, source_target_pairs={{1,0},{2,1},{3,2},{4,3},{5,4},{6,5},{7,6},{8,7},{9,8},{10,9},{11,1... | collective-permute-start | bytes 3080 | tf_op jit(solution)/shard_map/ppermute | solution.py:17
  374.0 5.7 %collective-permute-start.27 = (f32[256,1,130]{0,2,1:T(8,128)S(1)}, f32[256,1,130]{0,2,1:T(8,128)S(1)}, u32[]{:S(2)}, u32[]{:S(2)}) collective-permute-start(f32[256,1,130]{0,2,1:T(8,128)S(1)} %pad_maximum_fusion.1), channel_id=1, source_target_pairs={{32,0},{64,32},{96,64},{128,96},{160,128},{192,160},{224,192},{256... | collective-permute-start | bytes 399368 | tf_op jit(solution)/shard_map/ppermute | solution.py:17
  386.0 108.6 %all-reduce.4.cloned.1.call-done = f32[2,256,128]{2,1,0:T(8,128)} async-done(((f32[2,256,128]{2,1,0:T(8,128)}), f32[2,256,128]{2,1,0:T(8,128)}) %all-reduce.4.cloned.1.call-update) | async-done | bytes 262160 | tf_op jit(solution)/shard_map/psum | solution.py:153
  (186 shorter events, 123.5 us)
Async XLA Ops:
  7.2 487.4 %all-reduce.4.cloned.1.call-start = ((), (), s32[]{:S(2)}) async-start(), calls=%async_computation | async-start | bytes 524288 | tf_op jit(solution)/shard_map/psum | solution.py:153
  8.7 19.5 %collective-permute-start = (f32[256,1,1]{2,1,0:T(1,128)S(1)}, f32[256,1,1]{2,1,0:T(1,128)S(1)}, u32[]{:S(2)}, u32[]{:S(2)}) collective-permute-start(f32[256,1,1]{2,1,0:T(1,128)S(1)} %get-tuple-element.70), channel_id=1, source_target_pairs={{0,1},{1,2},{2,3},{3,4},{4,5},{5,6},{6,7},{7,8},{8,9},{9,10},{10,1... | collective-permute-start | bytes 3080 | tf_op jit(solution)/shard_map/ppermute | solution.py:16
  13.1 15.2 %collective-permute-start.1 = (f32[256,1,1]{2,1,0:T(1,128)S(1)}, f32[256,1,1]{2,1,0:T(1,128)S(1)}, u32[]{:S(2)}, u32[]{:S(2)}) collective-permute-start(f32[256,1,1]{2,1,0:T(1,128)S(1)} %get-tuple-element.71), channel_id=1, source_target_pairs={{1,0},{2,1},{3,2},{4,3},{5,4},{6,5},{7,6},{8,7},{9,8},{10,9},{11,1... | collective-permute-start | bytes 3080 | tf_op jit(solution)/shard_map/ppermute | solution.py:17
  26.1 22.5 %collective-permute-start.14 = (f32[2,256,1,128]{1,3,2,0:T(8,128)S(1)}, f32[2,256,1,128]{1,3,2,0:T(8,128)S(1)}, u32[]{:S(2)}, u32[]{:S(2)}) collective-permute-start(f32[2,256,1,128]{1,3,2,0:T(8,128)S(1)} %stack.165), channel_id=1, source_target_pairs={{0,16},{1,17},{2,18},{3,19},{4,20},{5,21},{6,22},{7,23},{8,24},{9,... | collective-permute-start | bytes 786440 | tf_op jit(solution)/shard_map/ppermute | solution.py:23
  43.8 11.5 %collective-permute-start.4 = (f32[2,256,1,128]{1,3,2,0:T(8,128)}, f32[2,256,1,128]{1,3,2,0:T(8,128)S(1)}, u32[]{:S(2)}, u32[]{:S(2)}) collective-permute-start(f32[2,256,1,128]{1,3,2,0:T(8,128)} %stack.148), channel_id=1, source_target_pairs={{0,16},{1,17},{2,18},{3,19},{4,20},{5,21},{6,22},{7,23},{8,24},{9,... | collective-permute-start | bytes 786440 | tf_op jit(solution)/shard_map/ppermute | solution.py:23
  56.4 35.1 %collective-permute-start.5 = (f32[2,256,1,128]{1,3,2,0:T(8,128)}, f32[2,256,1,128]{1,3,2,0:T(8,128)}, u32[]{:S(2)}, u32[]{:S(2)}) collective-permute-start(f32[2,256,1,128]{1,3,2,0:T(8,128)} %maximum_select_fusion), channel_id=1, source_target_pairs={{0,8},{1,9},{2,10},{3,11},{4,12},{5,13},{6,14},{7,15},{8,0},{9,1},... | collective-permute-start | bytes 786440 | tf_op jit(solution)/shard_map/ppermute | solution.py:23
  66.4 46.9 %collective-permute-start.15 = (f32[2,256,1,128]{1,3,2,0:T(8,128)}, f32[2,256,1,128]{1,3,2,0:T(8,128)}, u32[]{:S(2)}, u32[]{:S(2)}) collective-permute-start(f32[2,256,1,128]{1,3,2,0:T(8,128)} %maximum_select_fusion.10), channel_id=1, source_target_pairs={{0,8},{1,9},{2,10},{3,11},{4,12},{5,13},{6,14},{7,15},{8,0},{9,1},... | collective-permute-start | bytes 786440 | tf_op jit(solution)/shard_map/ppermute | solution.py:23
  115.6 40.6 %collective-permute-start.16 = (f32[2,256,1,128]{1,3,2,0:T(8,128)S(1)}, f32[2,256,1,128]{1,3,2,0:T(8,128)}, u32[]{:S(2)}, u32[]{:S(2)}) collective-permute-start(f32[2,256,1,128]{1,3,2,0:T(8,128)S(1)} %maximum_select_fusion.11), channel_id=1, source_target_pairs={{0,4},{1,5},{2,6},{3,7},{4,0},{5,1},{6,2},{7,3},{8,12},{9,13},{10,... | collective-permute-start | bytes 786440 | tf_op jit(solution)/shard_map/ppermute | solution.py:23
  118.7 43.2 %collective-permute-start.6 = (f32[2,256,1,128]{1,3,2,0:T(8,128)S(1)}, f32[2,256,1,128]{1,3,2,0:T(8,128)}, u32[]{:S(2)}, u32[]{:S(2)}) collective-permute-start(f32[2,256,1,128]{1,3,2,0:T(8,128)S(1)} %maximum_select_fusion.1), channel_id=1, source_target_pairs={{0,4},{1,5},{2,6},{3,7},{4,0},{5,1},{6,2},{7,3},{8,12},{9,13},{10,... | collective-permute-start | bytes 786440 | tf_op jit(solution)/shard_map/ppermute | solution.py:23
  164.0 17.5 %collective-permute-start.17 = (f32[2,256,1,128]{1,3,2,0:T(8,128)S(1)}, f32[2,256,1,128]{1,3,2,0:T(8,128)}, u32[]{:S(2)}, u32[]{:S(2)}) collective-permute-start(f32[2,256,1,128]{1,3,2,0:T(8,128)S(1)} %maximum_select_fusion.12), channel_id=1, source_target_pairs={{0,2},{1,3},{2,0},{3,1},{4,6},{5,7},{6,4},{7,5},{8,10},{9,11},{10,... | collective-permute-start | bytes 786440 | tf_op jit(solution)/shard_map/ppermute | solution.py:23
  167.0 20.2 %collective-permute-start.7 = (f32[2,256,1,128]{1,3,2,0:T(8,128)S(1)}, f32[2,256,1,128]{1,3,2,0:T(8,128)}, u32[]{:S(2)}, u32[]{:S(2)}) collective-permute-start(f32[2,256,1,128]{1,3,2,0:T(8,128)S(1)} %maximum_select_fusion.2), channel_id=1, source_target_pairs={{0,2},{1,3},{2,0},{3,1},{4,6},{5,7},{6,4},{7,5},{8,10},{9,11},{10,... | collective-permute-start | bytes 786440 | tf_op jit(solution)/shard_map/ppermute | solution.py:23
  189.3 9.4 %collective-permute-start.18 = (f32[2,256,1,128]{1,3,2,0:T(8,128)S(1)}, f32[2,256,1,128]{1,3,2,0:T(8,128)}, u32[]{:S(2)}, u32[]{:S(2)}) collective-permute-start(f32[2,256,1,128]{1,3,2,0:T(8,128)S(1)} %maximum_select_fusion.13), channel_id=1, source_target_pairs={{0,1},{1,0},{2,3},{3,2},{4,5},{5,4},{6,7},{7,6},{8,9},{9,8},{10,11... | collective-permute-start | bytes 786440 | tf_op jit(solution)/shard_map/ppermute | solution.py:23
  192.2 11.9 %collective-permute-start.8 = (f32[2,256,1,128]{1,3,2,0:T(8,128)S(1)}, f32[2,256,1,128]{1,3,2,0:T(8,128)S(1)}, u32[]{:S(2)}, u32[]{:S(2)}) collective-permute-start(f32[2,256,1,128]{1,3,2,0:T(8,128)S(1)} %maximum_select_fusion.3), channel_id=1, source_target_pairs={{0,1},{1,0},{2,3},{3,2},{4,5},{5,4},{6,7},{7,6},{8,9},{9,8},{10,11... | collective-permute-start | bytes 786440 | tf_op jit(solution)/shard_map/ppermute | solution.py:23
  217.5 11.7 %collective-permute-start.9 = (f32[2,256,1,128]{1,3,2,0:T(8,128)S(1)}, f32[2,256,1,128]{1,3,2,0:T(8,128)S(1)}, u32[]{:S(2)}, u32[]{:S(2)}) collective-permute-start(f32[2,256,1,128]{1,3,2,0:T(8,128)S(1)} %maximum_select_fusion.5), channel_id=1, source_target_pairs={{0,1},{1,0},{2,3},{3,2},{4,5},{5,4},{6,7},{7,6},{8,9},{9,8},{10,11... | collective-permute-start | bytes 786440 | tf_op jit(solution)/shard_map/ppermute | solution.py:23
  229.5 21.8 %collective-permute-start.10 = (f32[2,256,1,128]{1,3,2,0:T(8,128)S(1)}, f32[2,256,1,128]{1,3,2,0:T(8,128)S(1)}, u32[]{:S(2)}, u32[]{:S(2)}) collective-permute-start(f32[2,256,1,128]{1,3,2,0:T(8,128)S(1)} %maximum_select_fusion.6), channel_id=1, source_target_pairs={{0,2},{1,3},{2,0},{3,1},{4,6},{5,7},{6,4},{7,5},{8,10},{9,11},{10,... | collective-permute-start | bytes 786440 | tf_op jit(solution)/shard_map/ppermute | solution.py:23
  231.5 25.5 %collective-permute-start.20 = (f32[2,256,1,128]{1,3,2,0:T(8,128)S(1)}, f32[2,256,1,128]{1,3,2,0:T(8,128)S(1)}, u32[]{:S(2)}, u32[]{:S(2)}) collective-permute-start(f32[2,256,1,128]{1,3,2,0:T(8,128)S(1)} %maximum_select_fusion.16), channel_id=1, source_target_pairs={{0,2},{1,3},{2,0},{3,1},{4,6},{5,7},{6,4},{7,5},{8,10},{9,11},{10,... | collective-permute-start | bytes 786440 | tf_op jit(solution)/shard_map/ppermute | solution.py:23
  257.2 44.8 %collective-permute-start.11 = (f32[2,256,1,128]{1,3,2,0:T(8,128)S(1)}, f32[2,256,1,128]{1,3,2,0:T(8,128)S(1)}, u32[]{:S(2)}, u32[]{:S(2)}) collective-permute-start(f32[2,256,1,128]{1,3,2,0:T(8,128)S(1)} %maximum_select_fusion.7), channel_id=1, source_target_pairs={{0,4},{1,5},{2,6},{3,7},{4,0},{5,1},{6,2},{7,3},{8,12},{9,13},{10,... | collective-permute-start | bytes 786440 | tf_op jit(solution)/shard_map/ppermute | solution.py:23
  261.1 57.9 %collective-permute-start.21 = (f32[2,256,1,128]{1,3,2,0:T(8,128)S(1)}, f32[2,256,1,128]{1,3,2,0:T(8,128)S(1)}, u32[]{:S(2)}, u32[]{:S(2)}) collective-permute-start(f32[2,256,1,128]{1,3,2,0:T(8,128)S(1)} %maximum_select_fusion.17), channel_id=1, source_target_pairs={{0,4},{1,5},{2,6},{3,7},{4,0},{5,1},{6,2},{7,3},{8,12},{9,13},{10,... | collective-permute-start | bytes 786440 | tf_op jit(solution)/shard_map/ppermute | solution.py:23
  320.6 21.9 %collective-permute-start.12 = (f32[2,256,1,128]{1,3,2,0:T(8,128)}, f32[2,256,1,128]{1,3,2,0:T(8,128)}, u32[]{:S(2)}, u32[]{:S(2)}) collective-permute-start(f32[2,256,1,128]{1,3,2,0:T(8,128)} %maximum_select_fusion.8), channel_id=1, source_target_pairs={{0,8},{1,9},{2,10},{3,11},{4,12},{5,13},{6,14},{7,15},{8,0},{9,1},... | collective-permute-start | bytes 786440 | tf_op jit(solution)/shard_map/ppermute | solution.py:23
  331.6 18.0 %collective-permute-start.22 = (f32[2,256,1,128]{1,3,2,0:T(8,128)}, f32[2,256,1,128]{1,3,2,0:T(8,128)}, u32[]{:S(2)}, u32[]{:S(2)}) collective-permute-start(f32[2,256,1,128]{1,3,2,0:T(8,128)} %maximum_select_fusion.18), channel_id=1, source_target_pairs={{0,8},{1,9},{2,10},{3,11},{4,12},{5,13},{6,14},{7,15},{8,0},{9,1},... | collective-permute-start | bytes 786440 | tf_op jit(solution)/shard_map/ppermute | solution.py:23
  350.8 9.5 %collective-permute-start.23 = (f32[2,256,1,128]{1,3,2,0:T(8,128)S(1)}, f32[2,256,1,128]{1,3,2,0:T(8,128)}, u32[]{:S(2)}, u32[]{:S(2)}) collective-permute-start(f32[2,256,1,128]{1,3,2,0:T(8,128)S(1)} %maximum_select_fusion.19), channel_id=1, source_target_pairs={{0,16},{1,17},{2,18},{3,19},{4,20},{5,21},{6,22},{7,23},{8,24},{9,... | collective-permute-start | bytes 786440 | tf_op jit(solution)/shard_map/ppermute | solution.py:23
  353.5 19.7 %collective-permute-start.13 = (f32[2,256,1,128]{1,3,2,0:T(8,128)S(1)}, f32[2,256,1,128]{1,3,2,0:T(8,128)S(1)}, u32[]{:S(2)}, u32[]{:S(2)}) collective-permute-start(f32[2,256,1,128]{1,3,2,0:T(8,128)S(1)} %maximum_select_fusion.9), channel_id=1, source_target_pairs={{0,16},{1,17},{2,18},{3,19},{4,20},{5,21},{6,22},{7,23},{8,24},{9,... | collective-permute-start | bytes 786440 | tf_op jit(solution)/shard_map/ppermute | solution.py:23
  361.2 12.8 %collective-permute-start.24 = (f32[256,1,1]{0,2,1:T(1,128)S(1)}, f32[256,1,1]{0,2,1:T(1,128)S(1)}, u32[]{:S(2)}, u32[]{:S(2)}) collective-permute-start(f32[256,1,1]{0,2,1:T(1,128)S(1)} %get-tuple-element.62), channel_id=1, source_target_pairs={{0,1},{1,2},{2,3},{3,4},{4,5},{5,6},{6,7},{7,8},{8,9},{9,10},{10,1... | collective-permute-start | bytes 3080 | tf_op jit(solution)/shard_map/ppermute | solution.py:16
  363.1 10.9 %collective-permute-start.25 = (f32[256,1,1]{0,2,1:T(1,128)S(1)}, f32[256,1,1]{0,2,1:T(1,128)S(1)}, u32[]{:S(2)}, u32[]{:S(2)}) collective-permute-start(f32[256,1,1]{0,2,1:T(1,128)S(1)} %get-tuple-element.63), channel_id=1, source_target_pairs={{1,0},{2,1},{3,2},{4,3},{5,4},{6,5},{7,6},{8,7},{9,8},{10,9},{11,1... | collective-permute-start | bytes 3080 | tf_op jit(solution)/shard_map/ppermute | solution.py:17
  (28 other events, 608.3 us)
Sparse Core Ops, SparseCore 0:
  353.6 140.9 all-reduce.3
where the time goes:
time: 505 us; the launch traced here: 503 us
  waiting for transfers between devices  309 us (61%)
  starting transfers between devices  124 us (25%)
  other arithmetic  27 us (5%)
  matrix products  16.7 us (3%)
  between operations  15.3 us (3%)
  local copies, waits for them, and re-layouts  10.8 us (2%)
    ppermute x20, waiting for transfers between devices, partner(): lax.ppermute(array, axis, [(i, i ^ 1 << stride) for i in range(lax.axis_s...  200 us
    psum x1, waiting for transfers between devices, on_device(): filter_grad = lax.psum(local_grad, 'lat')  109 us
    ppermute x20, starting transfers between devices, partner(): lax.ppermute(array, axis, [(i, i ^ 1 << stride) for i in range(lax.axis_s...  83 us
    ppermute x4, starting transfers between devices, padded_2(): after = lax.ppermute(leading, axis, down)  29.6 us
    ppermute x4, starting transfers between devices, padded_2(): before = lax.ppermute(last, axis, up)  11.3 us
  transfers between devices with their start and end apart: 29, of which 20 were waited for; matrix products, arithmetic and copies ran while one was open for 6% of the time, Pallas kernels for 0%

commit v1 on v0

--- a/solution.py
+++ b/solution.py
@@ -150,7 +150,7 @@
         )
         / total_len
     )
-    filter_grad = lax.psum(local_grad, "lat")
+    filter_grad = jnp.sum(lax.all_gather(local_grad, "lat"), axis=0)
     flipped_taps = jnp.transpose(conv_weight[::-1, ::-1], (0, 1, 3, 2))
     input_grad = cotangent + apply_taps(with_rims(back_field), flipped_taps, lat_rows, columns)
     return (output, input_grad, filter_grad)

time: 505 us -> 407 us (0.81); the launches traced: 503 us -> 399 us
  waiting for transfers between devices: 309 us -> 209 us
    psum x1 -> x0, waiting for transfers between devices: 109 us -> none  [on_device(): filter_grad = lax.psum(local_grad, 'lat')]
    ppermute x4, waiting for transfers between devices: 1.13 us -> 11.7 us  [padded_2(): before = lax.ppermute(last, axis, up)]
    ppermute x4, starting transfers between devices: 29.6 us -> 23.9 us  [padded_2(): after = lax.ppermute(leading, axis, down)]
  transfers between devices with their start and end apart: 29 -> 29, of which waited for: 20 -> 21; matrix products, arithmetic and copies ran while one was open for 6% -> 8% of each run, Pallas kernels for 0% -> 0%
where the time goes in v1:
time: 407 us; the launch traced here: 399 us
  waiting for transfers between devices  209 us (51%)
  starting transfers between devices  120 us (29%)
  other arithmetic  29.6 us (7%)
  matrix products  16.1 us (4%)
  between operations  15.3 us (4%)
  local copies, waits for them, and re-layouts  9.51 us (2%)
    ppermute x20, waiting for transfers between devices, partner(): lax.ppermute(array, axis, [(i, i ^ 1 << stride) for i in range(lax.axis_s...  197 us
    ppermute x20, starting transfers between devices, partner(): lax.ppermute(array, axis, [(i, i ^ 1 << stride) for i in range(lax.axis_s...  86.5 us
    ppermute x4, starting transfers between devices, padded_2(): after = lax.ppermute(leading, axis, down)  23.9 us
    ppermute x4, waiting for transfers between devices, padded_2(): before = lax.ppermute(last, axis, up)  11.7 us
    ppermute x4, starting transfers between devices, padded_2(): before = lax.ppermute(last, axis, up)  9.17 us
    select_n x10, other arithmetic, forward_pairs(): data = jnp.where(upper, turned, data + other)  8.78 us
  transfers between devices with their start and end apart: 29, of which 21 were waited for; matrix products, arithmetic and copies ran while one was open for 8% of the time, Pallas kernels for 0%

profile of v1, /device:TPU:1, one launch (start us, length us, event | category | flops | bytes accessed | tf_op | source)
XLA Modules:
  0.0 399.2 jit_solution(2013626577380043928)
XLA Ops:
  8.4 5.5 %collective-permute-start.14 = (f32[2,256,1,128]{1,3,2,0:T(8,128)S(1)}, f32[2,256,1,128]{1,3,2,0:T(8,128)S(1)}, u32[]{:S(2)}, u32[]{:S(2)}) collective-permute-start(f32[2,256,1,128]{1,3,2,0:T(8,128)S(1)} %stack.165), channel_id=1, source_target_pairs={{0,16},{1,17},{2,18},{3,19},{4,20},{5,21},{6,22},{7,23},{8,24},{9,... | collective-permute-start | bytes 786440 | tf_op jit(solution)/shard_map/ppermute | solution.py:23
  15.2 11.1 %collective-permute-start.1 = (f32[256,1,1]{2,1,0:T(1,128)S(1)}, f32[256,1,1]{2,1,0:T(1,128)S(1)}, u32[]{:S(2)}, u32[]{:S(2)}) collective-permute-start(f32[256,1,1]{2,1,0:T(1,128)S(1)} %get-tuple-element.74), channel_id=1, source_target_pairs={{1,0},{2,1},{3,2},{4,3},{5,4},{6,5},{7,6},{8,7},{9,8},{10,9},{11,1... | collective-permute-start | bytes 3080 | tf_op jit(solution)/shard_map/ppermute | solution.py:17
  28.2 7.4 %collective-permute-done = f32[256,1,1]{2,1,0:T(1,128)S(1)} collective-permute-done((f32[256,1,1]{2,1,0:T(1,128)S(1)}, f32[256,1,1]{2,1,0:T(1,128)S(1)}, u32[]{:S(2)}, u32[]{:S(2)}) %collective-permute-start) | collective-permute-done | bytes 1056 | tf_op jit(solution)/shard_map/ppermute | solution.py:16
  52.3 4.6 %collective-permute-start.4 = (f32[2,256,1,128]{1,3,2,0:T(8,128)}, f32[2,256,1,128]{1,3,2,0:T(8,128)S(1)}, u32[]{:S(2)}, u32[]{:S(2)}) collective-permute-start(f32[2,256,1,128]{1,3,2,0:T(8,128)} %stack.148), channel_id=1, source_target_pairs={{0,16},{1,17},{2,18},{3,19},{4,20},{5,21},{6,22},{7,23},{8,24},{9,... | collective-permute-start | bytes 786440 | tf_op jit(solution)/shard_map/ppermute | solution.py:23
  57.1 6.7 %collective-permute-done.4 = f32[2,256,1,128]{1,3,2,0:T(8,128)S(1)} collective-permute-done((f32[2,256,1,128]{1,3,2,0:T(8,128)}, f32[2,256,1,128]{1,3,2,0:T(8,128)S(1)}, u32[]{:S(2)}, u32[]{:S(2)}) %collective-permute-start.4) | collective-permute-done | bytes 262176 | tf_op jit(solution)/shard_map/ppermute | solution.py:23
  69.9 10.3 %collective-permute-start.5 = (f32[2,256,1,128]{1,3,2,0:T(8,128)}, f32[2,256,1,128]{1,3,2,0:T(8,128)}, u32[]{:S(2)}, u32[]{:S(2)}) collective-permute-start(f32[2,256,1,128]{1,3,2,0:T(8,128)} %maximum_select_fusion), channel_id=1, source_target_pairs={{0,8},{1,9},{2,10},{3,11},{4,12},{5,13},{6,14},{7,15},{8,0},{9,1},... | collective-permute-start | bytes 786440 | tf_op jit(solution)/shard_map/ppermute | solution.py:23
  80.2 35.4 %collective-permute-done.15 = f32[2,256,1,128]{1,3,2,0:T(8,128)} collective-permute-done((f32[2,256,1,128]{1,3,2,0:T(8,128)}, f32[2,256,1,128]{1,3,2,0:T(8,128)}, u32[]{:S(2)}, u32[]{:S(2)}) %collective-permute-start.15) | collective-permute-done | bytes 262176 | tf_op jit(solution)/shard_map/ppermute | solution.py:23
  126.5 7.3 %collective-permute-start.6 = (f32[2,256,1,128]{1,3,2,0:T(8,128)S(1)}, f32[2,256,1,128]{1,3,2,0:T(8,128)}, u32[]{:S(2)}, u32[]{:S(2)}) collective-permute-start(f32[2,256,1,128]{1,3,2,0:T(8,128)S(1)} %maximum_select_fusion.1), channel_id=1, source_target_pairs={{0,4},{1,5},{2,6},{3,7},{4,0},{5,1},{6,2},{7,3},{8,12},{9,13},{10,... | collective-permute-start | bytes 786440 | tf_op jit(solution)/shard_map/ppermute | solution.py:23
  133.9 22.2 %collective-permute-done.16 = f32[2,256,1,128]{1,3,2,0:T(8,128)} collective-permute-done((f32[2,256,1,128]{1,3,2,0:T(8,128)S(1)}, f32[2,256,1,128]{1,3,2,0:T(8,128)}, u32[]{:S(2)}, u32[]{:S(2)}) %collective-permute-start.16) | collective-permute-done | bytes 262176 | tf_op jit(solution)/shard_map/ppermute | solution.py:23
  157.1 4.6 %collective-permute-done.6 = f32[2,256,1,128]{1,3,2,0:T(8,128)} collective-permute-done((f32[2,256,1,128]{1,3,2,0:T(8,128)S(1)}, f32[2,256,1,128]{1,3,2,0:T(8,128)}, u32[]{:S(2)}, u32[]{:S(2)}) %collective-permute-start.6) | collective-permute-done | bytes 262176 | tf_op jit(solution)/shard_map/ppermute | solution.py:23
  171.1 11.8 %collective-permute-done.17 = f32[2,256,1,128]{1,3,2,0:T(8,128)} collective-permute-done((f32[2,256,1,128]{1,3,2,0:T(8,128)S(1)}, f32[2,256,1,128]{1,3,2,0:T(8,128)}, u32[]{:S(2)}, u32[]{:S(2)}) %collective-permute-start.17) | collective-permute-done | bytes 262176 | tf_op jit(solution)/shard_map/ppermute | solution.py:23
  183.9 4.5 %collective-permute-done.7 = f32[2,256,1,128]{1,3,2,0:T(8,128)S(1)} collective-permute-done((f32[2,256,1,128]{1,3,2,0:T(8,128)S(1)}, f32[2,256,1,128]{1,3,2,0:T(8,128)S(1)}, u32[]{:S(2)}, u32[]{:S(2)}) %collective-permute-start.7) | collective-permute-done | bytes 262176 | tf_op jit(solution)/shard_map/ppermute | solution.py:23
  226.5 4.6 %collective-permute-done.19 = f32[2,256,1,128]{1,3,2,0:T(8,128)} collective-permute-done((f32[2,256,1,128]{1,3,2,0:T(8,128)}, f32[2,256,1,128]{1,3,2,0:T(8,128)}, u32[]{:S(2)}, u32[]{:S(2)}) %collective-permute-start.19) | collective-permute-done | bytes 262176 | tf_op jit(solution)/shard_map/ppermute | solution.py:23
  239.1 15.6 %collective-permute-done.10 = f32[2,256,1,128]{1,3,2,0:T(8,128)S(1)} collective-permute-done((f32[2,256,1,128]{1,3,2,0:T(8,128)S(1)}, f32[2,256,1,128]{1,3,2,0:T(8,128)S(1)}, u32[]{:S(2)}, u32[]{:S(2)}) %collective-permute-start.10) | collective-permute-done | bytes 262176 | tf_op jit(solution)/shard_map/ppermute | solution.py:23
  254.8 5.6 %collective-permute-done.20 = f32[2,256,1,128]{1,3,2,0:T(8,128)S(1)} collective-permute-done((f32[2,256,1,128]{1,3,2,0:T(8,128)S(1)}, f32[2,256,1,128]{1,3,2,0:T(8,128)S(1)}, u32[]{:S(2)}, u32[]{:S(2)}) %collective-permute-start.20) | collective-permute-done | bytes 262176 | tf_op jit(solution)/shard_map/ppermute | solution.py:23
  262.8 7.1 %collective-permute-start.21 = (f32[2,256,1,128]{1,3,2,0:T(8,128)S(1)}, f32[2,256,1,128]{1,3,2,0:T(8,128)S(1)}, u32[]{:S(2)}, u32[]{:S(2)}) collective-permute-start(f32[2,256,1,128]{1,3,2,0:T(8,128)S(1)} %maximum_select_fusion.17), channel_id=1, source_target_pairs={{0,4},{1,5},{2,6},{3,7},{4,0},{5,1},{6,2},{7,3},{8,12},{9,13},{10,... | collective-permute-start | bytes 786440 | tf_op jit(solution)/shard_map/ppermute | solution.py:23
  269.9 35.5 %collective-permute-done.11 = f32[2,256,1,128]{1,3,2,0:T(8,128)S(1)} collective-permute-done((f32[2,256,1,128]{1,3,2,0:T(8,128)S(1)}, f32[2,256,1,128]{1,3,2,0:T(8,128)S(1)}, u32[]{:S(2)}, u32[]{:S(2)}) %collective-permute-start.11) | collective-permute-done | bytes 262176 | tf_op jit(solution)/shard_map/ppermute | solution.py:23
  305.4 17.0 %collective-permute-done.21 = f32[2,256,1,128]{1,3,2,0:T(8,128)S(1)} collective-permute-done((f32[2,256,1,128]{1,3,2,0:T(8,128)S(1)}, f32[2,256,1,128]{1,3,2,0:T(8,128)S(1)}, u32[]{:S(2)}, u32[]{:S(2)}) %collective-permute-start.21) | collective-permute-done | bytes 262176 | tf_op jit(solution)/shard_map/ppermute | solution.py:23
  322.6 8.9 %collective-permute-start.12 = (f32[2,256,1,128]{1,3,2,0:T(8,128)S(1)}, f32[2,256,1,128]{1,3,2,0:T(8,128)S(1)}, u32[]{:S(2)}, u32[]{:S(2)}) collective-permute-start(f32[2,256,1,128]{1,3,2,0:T(8,128)S(1)} %maximum_select_fusion.8), channel_id=1, source_target_pairs={{0,8},{1,9},{2,10},{3,11},{4,12},{5,13},{6,14},{7,15},{8,0},{9,1},... | collective-permute-start | bytes 786440 | tf_op jit(solution)/shard_map/ppermute | solution.py:23
  331.5 5.1 %collective-permute-start.22 = (f32[2,256,1,128]{1,3,2,0:T(8,128)S(1)}, f32[2,256,1,128]{1,3,2,0:T(8,128)S(1)}, u32[]{:S(2)}, u32[]{:S(2)}) collective-permute-start(f32[2,256,1,128]{1,3,2,0:T(8,128)S(1)} %maximum_select_fusion.18), channel_id=1, source_target_pairs={{0,8},{1,9},{2,10},{3,11},{4,12},{5,13},{6,14},{7,15},{8,0},{9,1},... | collective-permute-start | bytes 786440 | tf_op jit(solution)/shard_map/ppermute | solution.py:23
  336.7 12.8 %collective-permute-done.12 = f32[2,256,1,128]{1,3,2,0:T(8,128)S(1)} collective-permute-done((f32[2,256,1,128]{1,3,2,0:T(8,128)S(1)}, f32[2,256,1,128]{1,3,2,0:T(8,128)S(1)}, u32[]{:S(2)}, u32[]{:S(2)}) %collective-permute-start.12) | collective-permute-done | bytes 262176 | tf_op jit(solution)/shard_map/ppermute | solution.py:23
  349.5 5.6 %collective-permute-done.22 = f32[2,256,1,128]{1,3,2,0:T(8,128)S(1)} collective-permute-done((f32[2,256,1,128]{1,3,2,0:T(8,128)S(1)}, f32[2,256,1,128]{1,3,2,0:T(8,128)S(1)}, u32[]{:S(2)}, u32[]{:S(2)}) %collective-permute-start.22) | collective-permute-done | bytes 262176 | tf_op jit(solution)/shard_map/ppermute | solution.py:23
  359.2 4.7 %collective-permute-start.13 = (f32[2,256,1,128]{1,3,2,0:T(8,128)S(1)}, f32[2,256,1,128]{1,3,2,0:T(8,128)S(1)}, u32[]{:S(2)}, u32[]{:S(2)}) collective-permute-start(f32[2,256,1,128]{1,3,2,0:T(8,128)S(1)} %maximum_select_fusion.9), channel_id=1, source_target_pairs={{0,16},{1,17},{2,18},{3,19},{4,20},{5,21},{6,22},{7,23},{8,24},{9,... | collective-permute-start | bytes 786440 | tf_op jit(solution)/shard_map/ppermute | solution.py:23
  377.8 5.5 %collective-permute-start.27 = (f32[256,1,130]{0,2,1:T(8,128)S(1)}, f32[256,1,130]{0,2,1:T(8,128)S(1)}, u32[]{:S(2)}, u32[]{:S(2)}) collective-permute-start(f32[256,1,130]{0,2,1:T(8,128)S(1)} %pad_maximum_fusion.1), channel_id=1, source_target_pairs={{32,0},{64,32},{96,64},{128,96},{160,128},{192,160},{224,192},{256... | collective-permute-start | bytes 399368 | tf_op jit(solution)/shard_map/ppermute | solution.py:17
  (176 shorter events, 124.9 us)
Async XLA Ops:
  7.2 382.1 %all-gather.2.cloned.1.call-start = ((), (), s32[]{:S(2)}) async-start(), calls=%async_computation | async-start | bytes 4456448 | tf_op jit(solution)/shard_map/all_gather | solution.py:153
  8.4 48.7 %collective-permute-start.14 = (f32[2,256,1,128]{1,3,2,0:T(8,128)S(1)}, f32[2,256,1,128]{1,3,2,0:T(8,128)S(1)}, u32[]{:S(2)}, u32[]{:S(2)}) collective-permute-start(f32[2,256,1,128]{1,3,2,0:T(8,128)S(1)} %stack.165), channel_id=1, source_target_pairs={{0,16},{1,17},{2,18},{3,19},{4,20},{5,21},{6,22},{7,23},{8,24},{9,... | collective-permute-start | bytes 786440 | tf_op jit(solution)/shard_map/ppermute | solution.py:23
  15.2 13.0 %collective-permute-start.1 = (f32[256,1,1]{2,1,0:T(1,128)S(1)}, f32[256,1,1]{2,1,0:T(1,128)S(1)}, u32[]{:S(2)}, u32[]{:S(2)}) collective-permute-start(f32[256,1,1]{2,1,0:T(1,128)S(1)} %get-tuple-element.74), channel_id=1, source_target_pairs={{1,0},{2,1},{3,2},{4,3},{5,4},{6,5},{7,6},{8,7},{9,8},{10,9},{11,1... | collective-permute-start | bytes 3080 | tf_op jit(solution)/shard_map/ppermute | solution.py:17
  26.3 9.3 %collective-permute-start = (f32[256,1,1]{2,1,0:T(1,128)S(1)}, f32[256,1,1]{2,1,0:T(1,128)S(1)}, u32[]{:S(2)}, u32[]{:S(2)}) collective-permute-start(f32[256,1,1]{2,1,0:T(1,128)S(1)} %get-tuple-element.73), channel_id=1, source_target_pairs={{0,1},{1,2},{2,3},{3,4},{4,5},{5,6},{6,7},{7,8},{8,9},{9,10},{10,1... | collective-permute-start | bytes 3080 | tf_op jit(solution)/shard_map/ppermute | solution.py:16
  37.4 9.7 %collective-permute-start.3 = (f32[256,1,130]{2,1,0:T(1,128)S(1)}, f32[256,1,130]{2,1,0:T(1,128)S(1)}, u32[]{:S(2)}, u32[]{:S(2)}) collective-permute-start(f32[256,1,130]{2,1,0:T(1,128)S(1)} %pad_maximum_fusion), channel_id=1, source_target_pairs={{32,0},{64,32},{96,64},{128,96},{160,128},{192,160},{224,192},{256... | collective-permute-start | bytes 399368 | tf_op jit(solution)/shard_map/ppermute | solution.py:17
  52.3 11.5 %collective-permute-start.4 = (f32[2,256,1,128]{1,3,2,0:T(8,128)}, f32[2,256,1,128]{1,3,2,0:T(8,128)S(1)}, u32[]{:S(2)}, u32[]{:S(2)}) collective-permute-start(f32[2,256,1,128]{1,3,2,0:T(8,128)} %stack.148), channel_id=1, source_target_pairs={{0,16},{1,17},{2,18},{3,19},{4,20},{5,21},{6,22},{7,23},{8,24},{9,... | collective-permute-start | bytes 786440 | tf_op jit(solution)/shard_map/ppermute | solution.py:23
  65.4 50.2 %collective-permute-start.15 = (f32[2,256,1,128]{1,3,2,0:T(8,128)}, f32[2,256,1,128]{1,3,2,0:T(8,128)}, u32[]{:S(2)}, u32[]{:S(2)}) collective-permute-start(f32[2,256,1,128]{1,3,2,0:T(8,128)} %maximum_select_fusion.10), channel_id=1, source_target_pairs={{0,8},{1,9},{2,10},{3,11},{4,12},{5,13},{6,14},{7,15},{8,0},{9,1},... | collective-permute-start | bytes 786440 | tf_op jit(solution)/shard_map/ppermute | solution.py:23
  69.9 51.4 %collective-permute-start.5 = (f32[2,256,1,128]{1,3,2,0:T(8,128)}, f32[2,256,1,128]{1,3,2,0:T(8,128)}, u32[]{:S(2)}, u32[]{:S(2)}) collective-permute-start(f32[2,256,1,128]{1,3,2,0:T(8,128)} %maximum_select_fusion), channel_id=1, source_target_pairs={{0,8},{1,9},{2,10},{3,11},{4,12},{5,13},{6,14},{7,15},{8,0},{9,1},... | collective-permute-start | bytes 786440 | tf_op jit(solution)/shard_map/ppermute | solution.py:23
  123.5 32.6 %collective-permute-start.16 = (f32[2,256,1,128]{1,3,2,0:T(8,128)S(1)}, f32[2,256,1,128]{1,3,2,0:T(8,128)}, u32[]{:S(2)}, u32[]{:S(2)}) collective-permute-start(f32[2,256,1,128]{1,3,2,0:T(8,128)S(1)} %maximum_select_fusion.11), channel_id=1, source_target_pairs={{0,4},{1,5},{2,6},{3,7},{4,0},{5,1},{6,2},{7,3},{8,12},{9,13},{10,... | collective-permute-start | bytes 786440 | tf_op jit(solution)/shard_map/ppermute | solution.py:23
  126.5 35.2 %collective-permute-start.6 = (f32[2,256,1,128]{1,3,2,0:T(8,128)S(1)}, f32[2,256,1,128]{1,3,2,0:T(8,128)}, u32[]{:S(2)}, u32[]{:S(2)}) collective-permute-start(f32[2,256,1,128]{1,3,2,0:T(8,128)S(1)} %maximum_select_fusion.1), channel_id=1, source_target_pairs={{0,4},{1,5},{2,6},{3,7},{4,0},{5,1},{6,2},{7,3},{8,12},{9,13},{10,... | collective-permute-start | bytes 786440 | tf_op jit(solution)/shard_map/ppermute | solution.py:23
  163.8 19.1 %collective-permute-start.17 = (f32[2,256,1,128]{1,3,2,0:T(8,128)S(1)}, f32[2,256,1,128]{1,3,2,0:T(8,128)}, u32[]{:S(2)}, u32[]{:S(2)}) collective-permute-start(f32[2,256,1,128]{1,3,2,0:T(8,128)S(1)} %maximum_select_fusion.12), channel_id=1, source_target_pairs={{0,2},{1,3},{2,0},{3,1},{4,6},{5,7},{6,4},{7,5},{8,10},{9,11},{10,... | collective-permute-start | bytes 786440 | tf_op jit(solution)/shard_map/ppermute | solution.py:23
  166.8 21.6 %collective-permute-start.7 = (f32[2,256,1,128]{1,3,2,0:T(8,128)S(1)}, f32[2,256,1,128]{1,3,2,0:T(8,128)S(1)}, u32[]{:S(2)}, u32[]{:S(2)}) collective-permute-start(f32[2,256,1,128]{1,3,2,0:T(8,128)S(1)} %maximum_select_fusion.2), channel_id=1, source_target_pairs={{0,2},{1,3},{2,0},{3,1},{4,6},{5,7},{6,4},{7,5},{8,10},{9,11},{10,... | collective-permute-start | bytes 786440 | tf_op jit(solution)/shard_map/ppermute | solution.py:23
  190.1 9.4 %collective-permute-start.18 = (f32[2,256,1,128]{1,3,2,0:T(8,128)S(1)}, f32[2,256,1,128]{1,3,2,0:T(8,128)}, u32[]{:S(2)}, u32[]{:S(2)}) collective-permute-start(f32[2,256,1,128]{1,3,2,0:T(8,128)S(1)} %maximum_select_fusion.13), channel_id=1, source_target_pairs={{0,1},{1,0},{2,3},{3,2},{4,5},{5,4},{6,7},{7,6},{8,9},{9,8},{10,11... | collective-permute-start | bytes 786440 | tf_op jit(solution)/shard_map/ppermute | solution.py:23
  193.1 11.9 %collective-permute-start.8 = (f32[2,256,1,128]{1,3,2,0:T(8,128)S(1)}, f32[2,256,1,128]{1,3,2,0:T(8,128)S(1)}, u32[]{:S(2)}, u32[]{:S(2)}) collective-permute-start(f32[2,256,1,128]{1,3,2,0:T(8,128)S(1)} %maximum_select_fusion.3), channel_id=1, source_target_pairs={{0,1},{1,0},{2,3},{3,2},{4,5},{5,4},{6,7},{7,6},{8,9},{9,8},{10,11... | collective-permute-start | bytes 786440 | tf_op jit(solution)/shard_map/ppermute | solution.py:23
  216.7 8.7 %collective-permute-start.9 = (f32[2,256,1,128]{1,3,2,0:T(8,128)}, f32[2,256,1,128]{1,3,2,0:T(8,128)}, u32[]{:S(2)}, u32[]{:S(2)}) collective-permute-start(f32[2,256,1,128]{1,3,2,0:T(8,128)} %maximum_select_fusion.5), channel_id=1, source_target_pairs={{0,1},{1,0},{2,3},{3,2},{4,5},{5,4},{6,7},{7,6},{8,9},{9,8},{10,11... | collective-permute-start | bytes 786440 | tf_op jit(solution)/shard_map/ppermute | solution.py:23
  219.7 11.3 %collective-permute-start.19 = (f32[2,256,1,128]{1,3,2,0:T(8,128)}, f32[2,256,1,128]{1,3,2,0:T(8,128)}, u32[]{:S(2)}, u32[]{:S(2)}) collective-permute-start(f32[2,256,1,128]{1,3,2,0:T(8,128)} %maximum_select_fusion.15), channel_id=1, source_target_pairs={{0,1},{1,0},{2,3},{3,2},{4,5},{5,4},{6,7},{7,6},{8,9},{9,8},{10,11... | collective-permute-start | bytes 786440 | tf_op jit(solution)/shard_map/ppermute | solution.py:23
  232.9 21.9 %collective-permute-start.10 = (f32[2,256,1,128]{1,3,2,0:T(8,128)S(1)}, f32[2,256,1,128]{1,3,2,0:T(8,128)S(1)}, u32[]{:S(2)}, u32[]{:S(2)}) collective-permute-start(f32[2,256,1,128]{1,3,2,0:T(8,128)S(1)} %maximum_select_fusion.6), channel_id=1, source_target_pairs={{0,2},{1,3},{2,0},{3,1},{4,6},{5,7},{6,4},{7,5},{8,10},{9,11},{10,... | collective-permute-start | bytes 786440 | tf_op jit(solution)/shard_map/ppermute | solution.py:23
  234.9 25.5 %collective-permute-start.20 = (f32[2,256,1,128]{1,3,2,0:T(8,128)S(1)}, f32[2,256,1,128]{1,3,2,0:T(8,128)S(1)}, u32[]{:S(2)}, u32[]{:S(2)}) collective-permute-start(f32[2,256,1,128]{1,3,2,0:T(8,128)S(1)} %maximum_select_fusion.16), channel_id=1, source_target_pairs={{0,2},{1,3},{2,0},{3,1},{4,6},{5,7},{6,4},{7,5},{8,10},{9,11},{10,... | collective-permute-start | bytes 786440 | tf_op jit(solution)/shard_map/ppermute | solution.py:23
  260.6 44.7 %collective-permute-start.11 = (f32[2,256,1,128]{1,3,2,0:T(8,128)S(1)}, f32[2,256,1,128]{1,3,2,0:T(8,128)S(1)}, u32[]{:S(2)}, u32[]{:S(2)}) collective-permute-start(f32[2,256,1,128]{1,3,2,0:T(8,128)S(1)} %maximum_select_fusion.7), channel_id=1, source_target_pairs={{0,4},{1,5},{2,6},{3,7},{4,0},{5,1},{6,2},{7,3},{8,12},{9,13},{10,... | collective-permute-start | bytes 786440 | tf_op jit(solution)/shard_map/ppermute | solution.py:23
  262.8 59.6 %collective-permute-start.21 = (f32[2,256,1,128]{1,3,2,0:T(8,128)S(1)}, f32[2,256,1,128]{1,3,2,0:T(8,128)S(1)}, u32[]{:S(2)}, u32[]{:S(2)}) collective-permute-start(f32[2,256,1,128]{1,3,2,0:T(8,128)S(1)} %maximum_select_fusion.17), channel_id=1, source_target_pairs={{0,4},{1,5},{2,6},{3,7},{4,0},{5,1},{6,2},{7,3},{8,12},{9,13},{10,... | collective-permute-start | bytes 786440 | tf_op jit(solution)/shard_map/ppermute | solution.py:23
  322.6 26.8 %collective-permute-start.12 = (f32[2,256,1,128]{1,3,2,0:T(8,128)S(1)}, f32[2,256,1,128]{1,3,2,0:T(8,128)S(1)}, u32[]{:S(2)}, u32[]{:S(2)}) collective-permute-start(f32[2,256,1,128]{1,3,2,0:T(8,128)S(1)} %maximum_select_fusion.8), channel_id=1, source_target_pairs={{0,8},{1,9},{2,10},{3,11},{4,12},{5,13},{6,14},{7,15},{8,0},{9,1},... | collective-permute-start | bytes 786440 | tf_op jit(solution)/shard_map/ppermute | solution.py:23
  331.5 23.5 %collective-permute-start.22 = (f32[2,256,1,128]{1,3,2,0:T(8,128)S(1)}, f32[2,256,1,128]{1,3,2,0:T(8,128)S(1)}, u32[]{:S(2)}, u32[]{:S(2)}) collective-permute-start(f32[2,256,1,128]{1,3,2,0:T(8,128)S(1)} %maximum_select_fusion.18), channel_id=1, source_target_pairs={{0,8},{1,9},{2,10},{3,11},{4,12},{5,13},{6,14},{7,15},{8,0},{9,1},... | collective-permute-start | bytes 786440 | tf_op jit(solution)/shard_map/ppermute | solution.py:23
  355.3 10.6 %collective-permute-start.23 = (f32[2,256,1,128]{1,3,2,0:T(8,128)S(1)}, f32[2,256,1,128]{1,3,2,0:T(8,128)}, u32[]{:S(2)}, u32[]{:S(2)}) collective-permute-start(f32[2,256,1,128]{1,3,2,0:T(8,128)S(1)} %maximum_select_fusion.19), channel_id=1, source_target_pairs={{0,16},{1,17},{2,18},{3,19},{4,20},{5,21},{6,22},{7,23},{8,24},{9,... | collective-permute-start | bytes 786440 | tf_op jit(solution)/shard_map/ppermute | solution.py:23
  359.2 14.2 %collective-permute-start.13 = (f32[2,256,1,128]{1,3,2,0:T(8,128)S(1)}, f32[2,256,1,128]{1,3,2,0:T(8,128)S(1)}, u32[]{:S(2)}, u32[]{:S(2)}) collective-permute-start(f32[2,256,1,128]{1,3,2,0:T(8,128)S(1)} %maximum_select_fusion.9), channel_id=1, source_target_pairs={{0,16},{1,17},{2,18},{3,19},{4,20},{5,21},{6,22},{7,23},{8,24},{9,... | collective-permute-start | bytes 786440 | tf_op jit(solution)/shard_map/ppermute | solution.py:23
  (23 other events, 478.5 us)
Sparse Core Ops, SparseCore 0:
  223.6 41.9 all-gather.1
